TPU v7x, 256 devices: a whole 4x4x8 slice. The times are simulated.
256 devices in a mesh: cell: 32 (over z_hi, x, core), mode: 8 (over z_lo, y).
Axes of the slice: x: 4, y: 4, z: 8 (z_hi: 4, z_lo: 2; z = z_hi * 2 + z_lo), core: 2. Of those that a mesh axis runs over, the one named last changes fastest.
Arguments:
- pod_modes: bfloat16 [3, 512, 4, 64, 128], P(None, 'mode', None, 'cell'), may hold values from -6 to 6
- slab_map: int32 [4, 64, 128], P(None, 'cell'), may hold values from 0 to 7
- slab_volume: float32 [8], replicated, may hold values from 0.25 to 4
- advect_index: int32 [8], replicated, may hold values from 0 to 511, as said below
- pair_adv: int32 [2048], replicated, may hold values from 0 to 7
- pair_mode: int32 [2048], replicated, may hold values from 0 to 511
- pair_amp: float32 [2048, 1024], replicated, may hold values from -0.2 to 0.2
Outputs:
- convective: float32 [512, 8, 512], P(('mode', 'cell'))
- response: float32 [512, 1024], P(('mode', 'cell'))
Inputs may be any that keep to these rules, and one draw needn't show every extreme that they name: `advect_index`: 8 distinct mode indices.
All inputs are finite; a program needn't handle non-finite values.
Results may differ from a plain program's by a relative error of at most 0.0043.
Values may be sent and summed in bfloat16 or wider, within the bound.
A program may use at most 128 MiB of HBM per device.

v0:
```python
import jax
import jax.numpy as jnp
from jax import lax
from jax.sharding import PartitionSpec as P


def split_up(x, dim, size):
    lengths = x.shape
    blocks = x.reshape(*lengths[:dim], size, lengths[dim] // size, *lengths[dim + 1 :])
    return jnp.moveaxis(blocks, dim, 0)


def sum_at_owner(x, axis, dim):
    blocks = split_up(x, dim, lax.axis_size(axis))
    arrived = lax.all_to_all(blocks, axis, split_axis=0, concat_axis=0, tiled=True)
    return arrived.sum(axis=0)


def padded(x, sides, width):
    for axis, dim in sides:
        size, length = (lax.axis_size(axis), x.shape[dim])
        up = [(i, (i + 1) % size) for i in range(size - 1)]
        down = [(j, i) for i, j in up]
        last = lax.slice_in_dim(x, length - width, length, axis=dim)
        first = lax.slice_in_dim(x, 0, width, axis=dim)
        before = lax.ppermute(last, axis, up)
        after = lax.ppermute(first, axis, down)
        x = jnp.concatenate([before, x, after], axis=dim)
    return x


def from_everyone(x, axis):
    copies = jnp.broadcast_to(x, (lax.axis_size(axis), *x.shape))
    return lax.all_to_all(copies, axis, split_axis=0, concat_axis=0, tiled=True)


def of_everyone(x, axis):
    everything = from_everyone(x, axis)
    return jnp.sum(everything.astype(jnp.float32), axis=0)


def gradients(haloed):
    interior = haloed[:, :, :, 1:-1].astype(jnp.float32)
    along_x = 0.5 * (jnp.roll(interior, -1, axis=2) - jnp.roll(interior, 1, axis=2))
    along_y = 0.5 * (
        haloed[:, :, :, 2:].astype(jnp.float32) - haloed[:, :, :, :-2].astype(jnp.float32)
    )
    along_z = 0.5 * (jnp.roll(interior, -1, axis=4) - jnp.roll(interior, 1, axis=4))
    return jnp.stack([along_x, along_y, along_z]).astype(jnp.bfloat16)


def contract(left_factor, grads):
    return jnp.einsum("ijdcxyz,dckxyz->ijk", left_factor, grads, preferred_element_type=jnp.float32)


def owner_rows(partial_value):
    return sum_at_owner(partial_value, "cell", 0)


def shards(pod_modes, slab_map, slab_volume, advect_index, pair_adv, pair_mode, pair_amp):
    mode_block = pod_modes.shape[1]
    planes = pod_modes.shape[2]
    rows_y = pod_modes.shape[3]
    cols_z = pod_modes.shape[4]
    mode_devs = lax.axis_size("mode")
    cell_devs = lax.axis_size("cell")
    mode_count = mode_block * mode_devs
    advect_count = advect_index.shape[0]
    scale_factor = float(planes * rows_y * cell_devs * cols_z) ** (-0.5)
    haloed = padded(pod_modes, (("cell", 3),), 1)
    first_mode = lax.axis_index("mode") * mode_block
    slots = lax.broadcasted_iota(jnp.int32, (advect_count, mode_block), 1)
    owned = (advect_index[:, None] == first_mode + slots).astype(jnp.bfloat16)
    picked = jnp.einsum("jm,cmxyz->cjxyz", owned, pod_modes, preferred_element_type=jnp.float32)
    chosen = of_everyone(picked.astype(jnp.bfloat16), "mode").astype(jnp.float32)
    levels = slab_volume.shape[0]
    level_ids = lax.broadcasted_iota(jnp.int32, (levels, planes, rows_y, cols_z), 0)
    volume = jnp.sum(
        jnp.where(slab_map[None] == level_ids, slab_volume[:, None, None, None], 0.0), axis=0
    )
    weighted = chosen * volume[None, None]
    left_factor = (
        jnp.transpose(pod_modes, (1, 0, 2, 3, 4))[:, None, None, :].astype(jnp.float32)
        * jnp.transpose(weighted, (1, 0, 2, 3, 4))[None, :, :, None]
    ).astype(jnp.bfloat16)
    local_grads = gradients(haloed)
    block_part = contract(left_factor, lax.all_gather(local_grads, "mode", axis=2, tiled=True))
    owned_rows = owner_rows(block_part)
    tensor = owned_rows * scale_factor
    flat_rows = tensor.reshape(tensor.shape[0], advect_count * mode_count)
    pair_slot = pair_adv * mode_count + pair_mode
    columns = jnp.take(flat_rows, pair_slot, axis=1)
    response = jnp.dot(
        columns, pair_amp, precision=lax.Precision.HIGHEST, preferred_element_type=jnp.float32
    )
    return (tensor, response)


def solution(mesh):
    in_specs = (P(None, "mode", None, "cell", None), P(None, "cell", None), P(), P(), P(), P(), P())
    out_specs = (P(("mode", "cell"), None, None), P(("mode", "cell"), None))
    return jax.shard_map(shards, mesh=mesh, in_specs=in_specs, out_specs=out_specs, check_vma=False)
```

profile of v0, /device:TPU:1, one launch (start us, length us, event | category | flops | bytes accessed | tf_op | source)
XLA Modules:
  0.0 197.5 jit_solution(4320587217358106295)
XLA Ops:
  7.2 0.0 all-gather.2.cloned.1.call-start
  7.2 1.2 convert_bitcast_fusion
  8.4 0.8 fusion.23
  9.2 5.1 %collective-permute-start = (bf16[3,64,4,1,128]{4,1,3,2,0:T(8,128)(2,1)}, bf16[3,64,4,1,128]{4,1,3,2,0:T(8,128)(2,1)}, u32[]{:S(2)}, u32[]{:S(2)}) collective-permute-start(bf16[3,64,4,1,128]{4,1,3,2,0:T(8,128)(2,1)} %get-tuple-element.13), channel_id=1, source_target_pairs={{8,0},{16,8},{24,16},{32,24},{40,32},{48,40},{56,48},{64,56},{72,6... | collective-permute-start | bytes 589832 | tf_op jit(solution)/shard_map/ppermute | solution.py:27
  14.3 1.9 collective-permute-start.1
  16.2 0.3 fusion.22
  16.5 1.2 slice_bitcast_fusion
  17.7 1.2 slice_bitcast_fusion.2
  18.9 0.8 slice_bitcast_fusion.4
  19.7 0.0 copy-start.3
  19.7 0.3 copy.49
  20.0 0.3 copy.50
  20.4 0.3 copy.51
  20.7 0.3 copy.52
  21.0 0.0 copy-start.4
  21.0 0.0 copy-start.5
  21.0 2.2 %fusion.9 = (bf16[1,3,64,4,2,128]{5,2,4,3,0,1:T(8,128)(2,1)S(1)}, bf16[1,3,64,4,2,128]{5,2,4,3,0,1:T(8,128)(2,1)S(1)}) fusion(f32[1,3,64,1,2,128]{5,2,4,3,1,0:T(8,128)} %get-tuple-element.3, f32[1,3,64,3,2,128]{5,2,4,3,1,0:T(8,128)} %get-tuple-element.5, f32[1,3,64,3,2,128]{5,2,4,3,0,1:T(8,128)} %get-tuple-element.4, ...), kind=kLoop, calls=%fused_computation.16 | loop fusion | flops 1966080 | bytes 3932160 | tf_op jit(solution)/shard_map/convert.1
  23.3 0.0 collective-permute-done
  23.3 0.0 collective-permute-done.1
  23.3 1.2 fusion.15
  24.5 1.2 pad_maximum_fusion
  25.6 0.0 all-gather.2.cloned.1.call-update
  25.7 0.0 copy-done.4
  25.7 1.2 fusion.4
  26.9 0.8 broadcast_in_dim.33
  27.8 4.9 %all-to-all-start = ((bf16[8,3,8,4,2,128]{5,2,4,3,1,0:T(8,128)(2,1)}), bf16[8,3,8,4,2,128]{5,2,4,3,1,0:T(8,128)(2,1)S(1)}, u32[]{:S(2)}, u32[]{:S(2)}) async-start(bf16[8,3,8,4,2,128]{5,2,4,3,1,0:T(8,128)(2,1)} %broadcast_in_dim.33), calls=%async_computation | async-start | bytes 786432 | tf_op jit(solution)/shard_map/all_to_all | solution.py:34
  32.7 0.6 copy.40
  33.3 0.0 copy-done.3
  33.3 0.0 copy-done.5
  33.3 0.1 select_reduce_fusion
  33.4 6.7 %all-to-all-done = bf16[8,3,8,4,2,128]{5,2,4,3,1,0:T(8,128)(2,1)S(1)} async-done(((bf16[8,3,8,4,2,128]{5,2,4,3,1,0:T(8,128)(2,1)}), bf16[8,3,8,4,2,128]{5,2,4,3,1,0:T(8,128)(2,1)S(1)}, u32[]{:S(2)}, u32[]{:S(2)}) %all-to-all-start) | async-done | bytes 393248 | tf_op jit(solution)/shard_map/all_to_all | solution.py:34
  40.1 0.1 convert_reduce_fusion
  40.2 0.0 copy-start.1
  40.2 0.0 copy-start.2
  40.2 94.3 %all-gather.2.cloned.1.call-done = bf16[3,3,512,4,2,128]{5,2,4,3,0,1:T(8,128)(2,1)} async-done(((bf16[3,3,64,4,2,128]{5,2,4,3,0,1:T(8,128)(2,1)}), bf16[3,3,512,4,2,128]{5,2,4,3,0,1:T(8,128)(2,1)}) %all-gather.2.cloned.1.call-update) | async-done | bytes 9437200 | tf_op jit(solution)/shard_map/all_gather | solution.py:87
  134.5 8.4 %fusion = f32[64,8,512,1,1,1,1]{2,1,6,0,5,4,3:T(8,128)} fusion(bf16[3,3,512,4,2,128]{5,2,4,3,0,1:T(8,128)(2,1)} %all-gather.2.cloned.1.call-done, f32[8,3,4,2,128]{4,0,3,2,1:T(8,128)S(1)} %multiply_bitcast_fusion, f32[64,3,4,2,128]{4,3,0,2,1:T(2,128)S(1)} %copy.40), kind=kOutput, calls=%fused_computation.2 | convolution fusion | flops 4841275392 | bytes 11370496 | tf_op jit(solution)/shard_map/ijdcxyz,dckxyz->ijk/dot_general | solution.py:53
  142.9 9.5 %all-to-all-start.1 = ((f32[32,2,8,512]{3,2,1,0:T(8,128)}), f32[32,2,8,512]{3,2,1,0:T(8,128)S(1)}, u32[]{:S(2)}, u32[]{:S(2)}) async-start(f32[32,2,8,512]{3,2,1,0:T(8,128)} %bitcast.22), calls=%async_computation.1 | async-start | bytes 2097152 | tf_op jit(solution)/shard_map/all_to_all | solution.py:15
  152.5 0.0 copy-done.1
  152.5 0.0 copy-done.2
  152.5 24.8 %all-to-all-done.1 = f32[32,2,8,512]{3,2,1,0:T(8,128)S(1)} async-done(((f32[32,2,8,512]{3,2,1,0:T(8,128)}), f32[32,2,8,512]{3,2,1,0:T(8,128)S(1)}, u32[]{:S(2)}, u32[]{:S(2)}) %all-to-all-start.1) | async-done | bytes 1048608 | tf_op jit(solution)/shard_map/all_to_all | solution.py:15
  177.3 0.1 reduce_sum.29
  177.4 0.0 copy-start
  177.4 0.6 copy.54
  178.0 5.5 %gather_fusion = f32[2048,2]{1,0:T(8,128)S(1)} fusion(f32[2,4096]{0,1:T(8,128)S(1)} %bitcast.57, s32[2048]{0:T(1024)S(1)} %broadcast_clamp_fusion), kind=kCustom, calls=%fused_computation | custom fusion | bytes 40960 | tf_op jit(solution)/shard_map/jit(_take)/gather | solution.py:92
  183.5 7.1 %fusion.5 = f32[2,1024]{1,0:T(2,128)} fusion(f32[2048,1024]{1,0:T(8,128)} %param.13, f32[2048,2]{1,0:T(8,128)S(1)} %gather_fusion, pred[2048]{0:T(1024)(128)(4,1)S(1)} %compare_and_fusion), kind=kOutput, calls=%fused_computation.9 | convolution fusion | flops 50335744 | bytes 8415232 | tf_op jit(solution)/shard_map/dot_general | solution.py:93
  190.7 0.0 copy-done
  (5 shorter events, 0.0 us)
Async XLA Ops:
  7.2 127.4 %all-gather.2.cloned.1.call-start = ((), (), s32[]{:S(2)}) async-start(), calls=%async_computation.2 | async-start | bytes 10616832 | tf_op jit(solution)/shard_map/all_gather | solution.py:87
  9.2 14.1 %collective-permute-start = (bf16[3,64,4,1,128]{4,1,3,2,0:T(8,128)(2,1)}, bf16[3,64,4,1,128]{4,1,3,2,0:T(8,128)(2,1)}, u32[]{:S(2)}, u32[]{:S(2)}) collective-permute-start(bf16[3,64,4,1,128]{4,1,3,2,0:T(8,128)(2,1)} %get-tuple-element.13), channel_id=1, source_target_pairs={{8,0},{16,8},{24,16},{32,24},{40,32},{48,40},{56,48},{64,56},{72,6... | collective-permute-start | bytes 589832 | tf_op jit(solution)/shard_map/ppermute | solution.py:27
  14.3 9.0 %collective-permute-start.1 = (bf16[3,64,4,1,128]{4,1,3,2,0:T(8,128)(2,1)}, bf16[3,64,4,1,128]{4,1,3,2,0:T(8,128)(2,1)}, u32[]{:S(2)}, u32[]{:S(2)}) collective-permute-start(bf16[3,64,4,1,128]{4,1,3,2,0:T(8,128)(2,1)} %get-tuple-element.14), channel_id=1, source_target_pairs={{0,8},{8,16},{16,24},{24,32},{32,40},{40,48},{48,56},{56,64},{64,7... | collective-permute-start | bytes 589832 | tf_op jit(solution)/shard_map/ppermute | solution.py:26
  19.7 13.6 %copy-start.3 = (s32[4,2,128]{2,1,0:T(2,128)S(1)}, s32[4,2,128]{2,1,0:T(2,128)}, u32[]{:S(2)}) copy-start(s32[4,2,128]{2,1,0:T(2,128)} %param.8) | copy-start | bytes 12292
  21.0 4.7 %copy-start.4 = (s32[8]{0:T(128)S(1)}, s32[8]{0:T(128)}, u32[]{:S(2)}) copy-start(s32[8]{0:T(128)} %param.10) | copy-start | bytes 100
  21.0 12.3 %copy-start.5 = (f32[8]{0:T(128)S(1)}, f32[8]{0:T(128)}, u32[]{:S(2)}) copy-start(f32[8]{0:T(128)} %param.9) | copy-start | bytes 100
  27.8 12.4 %all-to-all-start = ((bf16[8,3,8,4,2,128]{5,2,4,3,1,0:T(8,128)(2,1)}), bf16[8,3,8,4,2,128]{5,2,4,3,1,0:T(8,128)(2,1)S(1)}, u32[]{:S(2)}, u32[]{:S(2)}) async-start(bf16[8,3,8,4,2,128]{5,2,4,3,1,0:T(8,128)(2,1)} %broadcast_in_dim.33), calls=%async_computation | async-start | bytes 786432 | tf_op jit(solution)/shard_map/all_to_all | solution.py:34
  40.2 112.3 %copy-start.1 = (s32[2048]{0:T(1024)S(1)}, s32[2048]{0:T(1024)}, u32[]{:S(2)}) copy-start(s32[2048]{0:T(1024)} %param.12) | copy-start | bytes 24580
  40.2 112.3 %copy-start.2 = (s32[2048]{0:T(1024)S(1)}, s32[2048]{0:T(1024)}, u32[]{:S(2)}) copy-start(s32[2048]{0:T(1024)} %param.11) | copy-start | bytes 24580
  142.9 34.4 %all-to-all-start.1 = ((f32[32,2,8,512]{3,2,1,0:T(8,128)}), f32[32,2,8,512]{3,2,1,0:T(8,128)S(1)}, u32[]{:S(2)}, u32[]{:S(2)}) async-start(f32[32,2,8,512]{3,2,1,0:T(8,128)} %bitcast.22), calls=%async_computation.1 | async-start | bytes 2097152 | tf_op jit(solution)/shard_map/all_to_all | solution.py:15
  177.4 13.3 %copy-start = (f32[2,8,512]{2,1,0:T(8,128)}, f32[2,8,512]{2,1,0:T(8,128)S(1)}, u32[]{:S(2)}) copy-start(f32[2,8,512]{2,1,0:T(8,128)S(1)} %broadcast_multiply_fusion) | copy-start | bytes 98308
Sparse Core Ops, SparseCore 0:
  25.8 108.6 all-gather.1
where the time goes:
time: 201 us; the launch traced here: 198 us
  waiting for transfers between devices  126 us (63%)
  starting transfers between devices  21.5 us (11%)
  matrix products  16.8 us (8%)
  between operations  14.2 us (7%)
  local copies, waits for them, and re-layouts  13.1 us (7%)
  other arithmetic  6.06 us (3%)
    all_gather x1, waiting for transfers between devices, shards(): lax.all_gather(local_grads, 'mode', axis=2, tiled=True)  94.3 us
    all_to_all x1, waiting for transfers between devices, sum_at_owner(): lax.all_to_all(blocks, axis, split_axis=0, concat_axis=0, tiled=True)  24.8 us
    all_to_all x1, starting transfers between devices, sum_at_owner(): lax.all_to_all(blocks, axis, split_axis=0, concat_axis=0, tiled=True)  9.52 us
    dot_general x1, matrix products, contract(): jnp.einsum('ijdcxyz,dckxyz->ijk', left_factor, grads, preferred_element_t...  8.4 us
    dot_general x1, matrix products, shards(): jnp.dot(columns, pair_amp, precision=lax.Precision.HIGHEST, preferred_ele...  7.14 us
    all_to_all x1, waiting for transfers between devices, from_everyone(): return lax.all_to_all(copies, axis, split_axis=0, concat_axis=0, tiled=True)  6.71 us
    gather x1, local copies, waits for them, and re-layouts, shards(): columns = jnp.take(flat_rows, pair_slot, axis=1)  5.46 us
    ppermute x1, starting transfers between devices, padded(): after = lax.ppermute(first, axis, down)  5.1 us
  transfers between devices with their start and end apart: 5, of which 3 were waited for; matrix products, arithmetic and copies ran while one was open for 5% of the time, Pallas kernels for 0%

commit v1 on v0

v1 whole, which is shorter than its diff:
```python
import functools
import jax
import jax.numpy as jnp
from jax import lax
from jax.experimental import pallas as pl
from jax.experimental.pallas import tpu as pltpu
from jax.sharding import PartitionSpec as P

MESH = pl.DeviceIdType.MESH
F32 = jnp.float32
BF16 = jnp.bfloat16
NT = (((1,), (1,)), ((), ()))


def kernel(
    scale,
    u_ref, slab_ref, vol_ref, adv_ref, padv_ref, pmode_ref, amp_hbm,
    out_ref, resp_ref,
    blk, hal, up, um, q_ref,
    part, rs_buf, h_ref, hyh, hzp, hzm, v_ref,
    tf, tb, xbuf, zsrc, zbuf, fin,
    amp, amp_hi, amp_lo, onehot, mask,
    rs_s, rs_r, ag_s, ag_r, bulk_s, bulk_r, halo_s, halo_r, hy_s, hy_r, x_s, x_r, z_s, z_r, amp_sem,
):
    q = lax.axis_index("cell")
    m = lax.axis_index("mode")
    e = lax.rem(q, 8)
    zh = q // 8
    z = m // 4
    y = lax.rem(m, 4)
    ynext = lax.rem(y + 1, 4)
    yprev = lax.rem(y + 3, 4)
    yfar = lax.rem(y + 2, 4)
    qprev = lax.rem(q + 31, 32)
    qnext = lax.rem(q + 1, 32)

    def dev(cell, mode):
        return {"cell": cell, "mode": mode}

    def rcopy(src, dst, send, recv, target):
        return pltpu.make_async_remote_copy(
            src_ref=src, dst_ref=dst, send_sem=send, recv_sem=recv,
            device_id=target, device_id_type=MESH,
        )

    here = dev(q, m)
    m_ring = [lax.rem(m + t, 8) for t in range(8)]
    e_ring = [zh * 8 + lax.rem(e + t, 8) for t in range(8)]
    z_ring = [lax.rem(zh + t, 4) * 8 + e for t in range(4)]

    barrier = pltpu.get_barrier_semaphore()
    peers = [dev(q, m_ring[t]) for t in range(1, 8)]
    peers += [dev(e_ring[t], m) for t in range(1, 8)]
    peers += [dev(z_ring[t], m) for t in range(1, 4)]
    peers += [dev(qprev, m), dev(qnext, m)]
    for peer in peers:
        pl.semaphore_signal(barrier, inc=1, device_id=peer, device_id_type=MESH)
    amp_copy = pltpu.make_async_copy(amp_hbm, amp, amp_sem)
    amp_copy.start()

    sub = lax.broadcasted_iota(jnp.int32, (8, 64), 0)
    wanted = jnp.zeros((8, 64), jnp.int32)
    for j in range(8):
        wanted = jnp.where(sub == j, adv_ref[j], wanted)
    owned = (wanted == m * 64 + lax.broadcasted_iota(jnp.int32, (8, 64), 1)).astype(F32).astype(BF16)
    for row in range(2):
        picked = jnp.dot(owned, u_ref[row], preferred_element_type=F32)
        for d in range(3):
            for x in range(4):
                at = (d * 4 + x) * 128
                part[row * 4 + x, d] = picked[:, at : at + 128]
    pl.semaphore_wait(barrier, len(peers))

    rs = [None]
    for t in range(1, 8):
        copy = rcopy(part.at[m_ring[t]], rs_buf.at[t], rs_s.at[t], rs_r.at[t], dev(q, m_ring[t]))
        copy.start()
        rs.append(copy)

    up_y = dev(q, z * 4 + ynext)
    down_y = dev(q, z * 4 + yprev)
    to_z = dev(q, (1 - z) * 4 + y)

    def piece(ref, p):
        return ref.at[p // 2, pl.ds((p % 2) * 32, 32)]

    def move(src, slot, p, target):
        return rcopy(piece(src, p), piece(blk.at[slot], p), bulk_s.at[slot * 4 + p], bulk_r.at[slot * 4 + p], target)

    started = []

    def go(src, slot, p, target):
        copy = move(src, slot, p, target)
        copy.start()
        started.append(copy)

    def arrived(slot, p):
        move(u_ref, slot, p, here).wait_recv()

    def start_own(p):
        go(u_ref, 0, p, up_y)
        go(u_ref, 1, p, down_y)
        go(u_ref, 2, p, to_z)

    halo = [
        rcopy(u_ref.at[0], hal.at[1], halo_s.at[0], halo_r.at[0], dev(qprev, m)),
        rcopy(u_ref.at[1], hal.at[0], halo_s.at[1], halo_r.at[1], dev(qnext, m)),
    ]
    start_own(0)
    start_own(1)
    halo[0].start()
    halo[1].start()

    for x in range(4):
        for row in range(2):
            ids = slab_ref[x, row : row + 1, :]
            vol = jnp.zeros((1, 128), F32)
            for level in range(8):
                vol = jnp.where(ids == level, vol_ref[level], vol)
            v_ref[row * 4 + x : row * 4 + x + 1, :] = vol * (0.5 * scale)

    def shift(k, carry):
        at = pl.ds(pl.multiple_of(k * 128, 128), 128)
        for row in range(2):
            tile = u_ref[row, :, at].astype(F32)
            up[row, :, at] = pltpu.roll(tile, 127, 1).astype(BF16)
            um[row, :, at] = pltpu.roll(tile, 1, 1).astype(BF16)
        return carry

    lax.fori_loop(0, 12, shift, 0)

    total = part[m]
    for t in range(1, 8):
        rs[t].wait_recv()
        total = total + rs_buf[t]
    h_ref[m] = total * v_ref[pl.ds(m, 1), :][None]
    ag = [None]
    for t in range(1, 8):
        copy = rcopy(h_ref.at[m], h_ref.at[m], ag_s.at[t], ag_r.at[t], dev(q, m_ring[t]))
        copy.start()
        ag.append(copy)
    start_own(2)
    start_own(3)

    def pick_modes(k, carry):
        at = pl.ds(pl.multiple_of(k * 256, 256), 256)
        rows = lax.broadcasted_iota(jnp.int32, (512, 256), 0)
        onehot[:, at] = (rows == pmode_ref[:, at]).astype(F32).astype(BF16)
        return carry

    lax.fori_loop(0, 8, pick_modes, 0)
    mask[...] = (lax.broadcasted_iota(jnp.int32, (8, 2048), 0) == padv_ref[...]).astype(F32)

    for t in range(1, 8):
        ag[t].wait_recv()
    hy = [
        rcopy(h_ref.at[pl.ds(0, 4), 1], hyh.at[1], hy_s.at[0], hy_r.at[0], dev(qprev, m)),
        rcopy(h_ref.at[pl.ds(4, 4), 1], hyh.at[0], hy_s.at[1], hy_r.at[1], dev(qnext, m)),
    ]
    hy[0].start()
    hy[1].start()
    for n in range(8):
        hzp[n] = pltpu.roll(h_ref[n, 2], 127, 1)
        hzm[n] = pltpu.roll(h_ref[n, 2], 1, 1)

    def relay_z(p):
        arrived(2, p)
        go(blk.at[2], 3, p, up_y)
        go(blk.at[2], 4, p, down_y)

    for p in (0, 1):
        arrived(0, p)
        go(blk.at[0], 5, p, up_y)
        relay_z(p)
    for p in (2, 3):
        arrived(1, p)
        go(blk.at[1], 5, p, down_y)
        relay_z(p)

    halo[0].wait_recv()
    halo[1].wait_recv()
    hy[0].wait_recv()
    hy[1].wait_recv()

    first_ok = jnp.where(q == 0, 0.0, 1.0)
    last_ok = jnp.where(q == 31, 0.0, 1.0)

    def build(row, c, carry_in):
        def one(x, carry):
            xp = lax.rem(x + 1, 4)
            xm = lax.rem(x + 3, 4)
            at = pl.ds(pl.multiple_of((c * 4 + x) * 128, 128), 128)
            atp = pl.ds(pl.multiple_of((c * 4 + xp) * 128, 128), 128)
            atm = pl.ds(pl.multiple_of((c * 4 + xm) * 128, 128), 128)
            n = row * 4 + x
            for g in range(2):
                cut = pl.ds(g * 32, 32)
                uxp = u_ref[row, cut, atp].astype(F32)
                uxm = u_ref[row, cut, atm].astype(F32)
                uzp = up[row, cut, at].astype(F32)
                uzm = um[row, cut, at].astype(F32)
                if row == 0:
                    uyp = u_ref[1, cut, at].astype(F32)
                    uym = hal[0, cut, at].astype(F32) * first_ok
                else:
                    uyp = hal[1, cut, at].astype(F32) * last_ok
                    uym = u_ref[0, cut, at].astype(F32)
                for j in range(8):
                    js = slice(j, j + 1)
                    hyp = h_ref[4 + x, 1, js] if row == 0 else hyh[1, x, js]
                    hym = hyh[0, x, js] if row == 0 else h_ref[x, 1, js]
                    qq = h_ref[row * 4 + xm, 0, js] * uxm - h_ref[row * 4 + xp, 0, js] * uxp
                    qq = qq + (hym * uym - hyp * uyp)
                    qq = qq + (hzm[n, js] * uzm - hzp[n, js] * uzp)
                    lines = pl.ds(j * 64 + g * 32, 32)
                    q_ref[row, lines, at] = qq.astype(BF16)
            return carry

        return lax.fori_loop(0, 4, one, carry_in)

    for row in range(2):
        lax.fori_loop(0, 3, functools.partial(build, row), 0)
        for p in (2 * row, 2 * row + 1):
            arrived(5, p)
            go(blk.at[5], 6, p, to_z)

    def send_batch(n):
        tb[n] = tf[...].astype(BF16).reshape(4, 8, 16, 128)
        for t in range(1, 8):
            x_copy(n, t).start()

    def x_copy(n, t):
        return rcopy(
            tb.at[n, :, lax.rem(e + t, 8)], xbuf.at[n, t], x_s.at[n, t], x_r.at[n, t], dev(e_ring[t], m)
        )

    def products(n, low, high):
        total = None
        for r in range(2):
            pair = jnp.concatenate([low[r], high[r]], axis=0)
            value = lax.dot_general(q_ref[r], pair, NT, preferred_element_type=F32)
            total = value if total is None else total + value
        for j in range(8):
            tf[pl.ds(j, 64, stride=8), :] = total[j * 64 : (j + 1) * 64]
        send_batch(n)

    def z_copy(n, t):
        return rcopy(zsrc.at[n, lax.rem(zh + t, 4)], zbuf.at[n, t], z_s.at[n, t], z_r.at[n, t], dev(z_ring[t], m))

    def gather_batch(n):
        total = tb[n, :, e].astype(F32)
        for t in range(1, 8):
            x_copy(n, t).wait_recv()
            total = total + xbuf[n, t].astype(F32)
        zsrc[n] = total
        for t in range(1, 4):
            z_copy(n, t).start()

    products(0, u_ref, blk.at[2])
    for p in range(2):
        arrived(0, 2 + p)
        arrived(1, p)
    products(1, blk.at[0], blk.at[1])
    gather_batch(0)

    amp_copy.wait()

    def split_amp(k, carry):
        at = pl.ds(pl.multiple_of(k * 32, 32), 32)
        value = amp[at]
        hi = value.astype(BF16)
        amp_hi[at] = hi
        amp_lo[at] = (value - hi.astype(F32)).astype(BF16)
        return carry

    lax.fori_loop(0, 64, split_amp, 0)
    gather_batch(1)
    for p in range(4):
        arrived(3, p)
        arrived(4, p)
    products(2, blk.at[3], blk.at[4])
    gather_batch(2)
    for p in range(4):
        arrived(6, p)
    products(3, blk.at[5], blk.at[6])
    gather_batch(3)

    blocks = [
        (m, (1 - z) * 4 + y),
        (z * 4 + yprev, z * 4 + ynext),
        ((1 - z) * 4 + yprev, (1 - z) * 4 + ynext),
        (z * 4 + yfar, (1 - z) * 4 + yfar),
    ]
    for n in range(4):
        value = zsrc[n, zh]
        for t in range(1, 4):
            z_copy(n, t).wait_recv()
            value = value + zbuf[n, t]
        fin[blocks[n][0]] = value
        fin[blocks[n][1]] = pltpu.roll(value, 64, 1)

    low = lax.broadcasted_iota(jnp.int32, (16, 128), 1) < 64
    columns = []
    for t in range(4):
        columns.append(jnp.where(low, fin[2 * t], pltpu.roll(fin[2 * t + 1], 64, 1)))
    tensor = jnp.concatenate(columns, axis=1)
    out_ref[...] = tensor
    top = tensor.astype(BF16)
    rest = (tensor - top.astype(F32)).astype(BF16)
    chosen = jnp.dot(jnp.concatenate([top, rest], axis=0), onehot[...], preferred_element_type=F32)
    chosen = chosen[:16] + chosen[16:]
    first = jnp.sum(chosen[:8] * mask[...], axis=0, keepdims=True)
    second = jnp.sum(chosen[8:] * mask[...], axis=0, keepdims=True)
    rows = lax.broadcasted_iota(jnp.int32, (16, 2048), 0)
    both = jnp.where(lax.rem(rows, 2) == 0, first, second)
    both_hi = both.astype(BF16).astype(F32)
    stacked = jnp.where(rows < 2, both_hi, jnp.where(rows < 4, both - both_hi, 0.0)).astype(BF16)
    answer = jnp.dot(stacked, amp_hi[...], preferred_element_type=F32)
    answer = answer + jnp.dot(stacked, amp_lo[...], preferred_element_type=F32)
    resp_ref[...] = answer[0:2] + answer[2:4]

    for t in range(1, 8):
        rs[t].wait_send()
        ag[t].wait_send()
    for copy in started + halo + hy:
        copy.wait_send()
    for n in range(4):
        for t in range(1, 8):
            x_copy(n, t).wait_send()
        for t in range(1, 4):
            z_copy(n, t).wait_send()


def shards(pod_modes, slab_map, slab_volume, advect_index, pair_adv, pair_mode, pair_amp):
    cells = pod_modes.shape[2] * pod_modes.shape[3] * lax.axis_size("cell") * pod_modes.shape[4]
    u = jnp.transpose(pod_modes, (3, 1, 0, 2, 4)).reshape(2, 64, 1536)
    vmem = pl.BlockSpec(memory_space=pltpu.VMEM)
    smem = pl.BlockSpec(memory_space=pltpu.SMEM)
    dma = pltpu.SemaphoreType.DMA
    tensor, response = pl.pallas_call(
        functools.partial(kernel, float(cells) ** -0.5),
        out_shape=(
            jax.ShapeDtypeStruct((16, 512), F32),
            jax.ShapeDtypeStruct((2, 1024), F32),
        ),
        in_specs=[vmem, vmem, smem, smem, vmem, vmem, pl.BlockSpec(memory_space=pl.ANY)],
        out_specs=(vmem, vmem),
        scratch_shapes=[
            pltpu.VMEM((7, 2, 64, 1536), BF16),
            pltpu.VMEM((2, 64, 1536), BF16),
            pltpu.VMEM((2, 64, 1536), BF16),
            pltpu.VMEM((2, 64, 1536), BF16),
            pltpu.VMEM((2, 512, 1536), BF16),
            pltpu.VMEM((8, 3, 8, 128), F32),
            pltpu.VMEM((8, 3, 8, 128), F32),
            pltpu.VMEM((8, 3, 8, 128), F32),
            pltpu.VMEM((2, 4, 8, 128), F32),
            pltpu.VMEM((8, 8, 128), F32),
            pltpu.VMEM((8, 8, 128), F32),
            pltpu.VMEM((8, 128), F32),
            pltpu.VMEM((512, 128), F32),
            pltpu.VMEM((4, 4, 8, 16, 128), BF16),
            pltpu.VMEM((4, 8, 4, 16, 128), BF16),
            pltpu.VMEM((4, 4, 16, 128), F32),
            pltpu.VMEM((4, 4, 16, 128), F32),
            pltpu.VMEM((8, 16, 128), F32),
            pltpu.VMEM((2048, 1024), F32),
            pltpu.VMEM((2048, 1024), BF16),
            pltpu.VMEM((2048, 1024), BF16),
            pltpu.VMEM((512, 2048), BF16),
            pltpu.VMEM((8, 2048), F32),
            dma((8,)), dma((8,)), dma((8,)), dma((8,)),
            dma((28,)), dma((28,)), dma((2,)), dma((2,)), dma((2,)), dma((2,)),
            dma((4, 8)), dma((4, 8)), dma((4, 4)), dma((4, 4)), dma,
        ],
        compiler_params=pltpu.CompilerParams(
            collective_id=0, has_side_effects=True, vmem_limit_bytes=60 * 2**20
        ),
        name="pod_tensor",
    )(
        u, slab_map, slab_volume, advect_index,
        pair_adv.reshape(1, -1), pair_mode.reshape(1, -1), pair_amp,
    )
    return tensor.reshape(2, 8, 512), response


def solution(mesh):
    in_specs = (P(None, "mode", None, "cell", None), P(None, "cell", None), P(), P(), P(), P(), P())
    out_specs = (P(("mode", "cell"), None, None), P(("mode", "cell"), None))
    return jax.shard_map(shards, mesh=mesh, in_specs=in_specs, out_specs=out_specs, check_vma=False)
```

time: 201 us -> 66.8 us (0.33); the launches traced: 198 us -> 66.6 us
  waiting for transfers between devices: 126 us -> 0 us
  Pallas kernels: 0 us -> 61.3 us
  starting transfers between devices: 21.5 us -> 0 us
  matrix products: 16.8 us -> 0 us
  between operations: 14.2 us -> 0.64 us
  local copies, waits for them, and re-layouts: 13.1 us -> 4.65 us
  other arithmetic: 6.06 us -> 0 us
    all_gather x1 -> x0, waiting for transfers between devices: 94.3 us -> none  [shards(): lax.all_gather(local_grads, 'mode', axis=2, tiled=True)]
    pallas_call x0 -> x1, Pallas kernels: none -> 61.3 us  [shards(): pl.pallas_call(functools.partial(kernel, float(cells) ** (-0.5)), out_sha...]
    all_to_all x2 -> x0, waiting for transfers between devices: 31.5 us -> none  [the longest x1 24.8 us: sum_at_owner(): lax.all_to_all(blocks, axis, split_axis=0, concat_axis=0, tiled=True)]
    dot_general x3 -> x0, matrix products: 16.8 us -> none  [the longest x1 8.4 us: contract(): jnp.einsum('ijdcxyz,dckxyz->ijk', left_factor, grads, preferred_element_t...]
    all_to_all x2 -> x0, starting transfers between devices: 14.5 us -> none  [the longest x1 9.52 us: sum_at_owner(): lax.all_to_all(blocks, axis, split_axis=0, concat_axis=0, tiled=True)]
    ppermute x2 -> x0, starting transfers between devices: 7.02 us -> none  [the longest x1 5.1 us: padded(): after = lax.ppermute(first, axis, down)]
    gather x1 -> x0, local copies, waits for them, and re-layouts: 5.46 us -> none  [shards(): columns = jnp.take(flat_rows, pair_slot, axis=1)]
    another operation x3 -> x0, other arithmetic: 4.57 us -> none  [the longest x2 2.33 us: gradients(): return jnp.stack([along_x, along_y, along_z]).astype(jnp.bfloat16)]
  transfers between devices with their start and end apart: 5 -> 0, of which waited for: 3 -> 0; matrix products, arithmetic and copies ran while one was open for 5% -> 0% of each run, Pallas kernels for 0% -> 0%
where the time goes in v1:
time: 66.8 us; the launch traced here: 66.6 us
  Pallas kernels  61.3 us (92%)
  local copies, waits for them, and re-layouts  4.65 us (7%)
    pallas_call x1, Pallas kernels, shards(): pl.pallas_call(functools.partial(kernel, float(cells) ** (-0.5)), out_sha...  61.3 us
    unnamed x2, local copies, waits for them, and re-layouts  2.67 us

profile of v1, /device:TPU:1, one launch (start us, length us, event | category | flops | bytes accessed | tf_op | source)
XLA Modules:
  0.0 66.6 jit_solution(4188666484097231426)
XLA Ops:
  0.6 1.1 %copy.9 = bf16[2,64,3,4,128]{4,3,2,1,0:T(4,128)(2,1)S(1)} copy(bf16[2,64,3,4,128]{4,0,3,1,2:T(2,128)(2,1)} %bitcast.4) | data formatting | bytes 786432 | tf_op jit(solution)/shard_map/transpose | solution.py:336
  1.7 0.9 %reshape.16.u_ref = bf16[2,64,1536]{2,1,0:T(8,128)(2,1)} reshape(bf16[2,64,3,4,128]{4,3,2,1,0:T(4,128)(2,1)S(1)} %copy.9) | data formatting | bytes 786432 | tf_op jit(solution)/shard_map/reshape | solution.py:336
  2.6 61.3 %pod_tensor.1 = (f32[16,512]{1,0:T(8,128)}, f32[2,1024]{1,0:T(2,128)}) custom-call(bf16[2,64,1536]{2,1,0:T(8,128)(2,1)} %reshape.16.u_ref, s32[4,2,128]{2,1,0:T(2,128)} %slab_ref.1, f32[8]{0:T(128)} %vol_ref.1, s32[8]{0:T(128)} %adv_ref.1, s32[1,2048]{1,0:T(1,128)} %bitcast.6, s32[1,2048]{1,0:T(1,128)} %bitcast.7, f32[2048,1024]{1,0:T(8,128)} %amp_hbm.1), custom_call_target="tpu_custom_call" | custom-call | tf_op jit(solution)/shard_map/pod_tensor/pallas_call | solution.py:340
  63.9 1.4 %copy.12 = f32[2,8,512]{2,1,0:T(8,128)} copy(f32[2,8,512]{2,1,0:T(8,128)} %bitcast.5) | data formatting | bytes 65536
  65.3 1.3 %copy.13 = f32[2,1024]{1,0:T(2,128)} copy(f32[2,1024]{1,0:T(2,128)} %get-tuple-element.9) | data formatting | bytes 16384

commit v2 on v1

v2 whole, which is shorter than its diff:
```python
import functools
import jax
import jax.numpy as jnp
from jax import lax
from jax.experimental import pallas as pl
from jax.experimental.pallas import tpu as pltpu
from jax.sharding import PartitionSpec as P

MESH = pl.DeviceIdType.MESH
F32 = jnp.float32
BF16 = jnp.bfloat16
NT = (((1,), (1,)), ((), ()))


def kernel(
    scale,
    u_ref, slab_ref, vol_ref, adv_ref, padv_ref, pmode_ref, amp_hbm,
    out_ref, resp_ref,
    ub, blk, hal, up, um, q_ref,
    part, rs_buf, h_ref, hyh, hzp, hzm,
    tf, tb, xbuf, zsrc, zbuf, fin,
    amp, amp_hi, amp_lo, onehot, mask,
    rs_s, rs_r, ag_s, ag_r, own_s, own_r, bulk_s, bulk_r, halo_s, halo_r, hy_s, hy_r, x_s, x_r, z_s, z_r, amp_sem,
):
    q = lax.axis_index("cell")
    m = lax.axis_index("mode")
    core = lax.rem(q, 2)
    e = lax.rem(q, 8)
    zh = q // 8
    z = m // 4
    y = lax.rem(m, 4)
    stays = core == z
    vq = q - core + z
    vm = core * 4 + y
    ynext = lax.rem(y + 1, 4)
    yprev = lax.rem(y + 3, 4)
    yfar = lax.rem(y + 2, 4)

    def place(cell, block):
        return dev(cell - lax.rem(cell, 2) + block // 4, lax.rem(cell, 2) * 4 + lax.rem(block, 4))

    def dev(cell, mode):
        return {"cell": cell, "mode": mode}

    def rcopy(src, dst, send, recv, target):
        return pltpu.make_async_remote_copy(
            src_ref=src, dst_ref=dst, send_sem=send, recv_sem=recv,
            device_id=target, device_id_type=MESH,
        )

    here = dev(q, m)
    n_ring = [lax.rem(vm + t, 8) for t in range(8)]
    e_ring = [lax.rem(e + t, 8) for t in range(8)]
    z_ring = [lax.rem(zh + t, 4) * 8 + e for t in range(4)]
    vprev = lax.rem(vq + 31, 32)
    vnext = lax.rem(vq + 1, 32)
    qprev = lax.rem(q + 31, 32)
    qnext = lax.rem(q + 1, 32)

    barrier = pltpu.get_barrier_semaphore()
    y_of = [lax.rem(y + t, 4) for t in range(4)]
    peers = [place(vq, n_ring[t]) for t in range(1, 8)]
    peers += [dev(vq, lax.rem(z + t // 4, 2) * 4 + y_of[t % 4]) for t in range(1, 8)]
    peers += [
        dev(zh * 8 + lax.rem(e // 2 + t // 2, 4) * 2 + z, lax.rem(z + t, 2) * 4 + y) for t in range(1, 8)
    ]
    peers += [dev(z_ring[t], m) for t in range(1, 4)]
    peers += [dev(vprev, vm), dev(vnext, vm)]
    peers += [place(vnext, x) for x in range(4)] + [place(vprev, 4 + x) for x in range(4)]

    def greet(peer, times):
        pl.semaphore_signal(barrier, inc=times, device_id=peer, device_id_type=MESH)

    for peer in peers:
        greet(peer, 1)

    @pl.when(jnp.logical_not(stays))
    def _():
        greet(dev(vq, m), 2)

    amp_copy = pltpu.make_async_copy(amp_hbm, amp, amp_sem)
    amp_copy.start()

    sub = lax.broadcasted_iota(jnp.int32, (8, 64), 0)
    wanted = jnp.zeros((8, 64), jnp.int32)
    for j in range(8):
        wanted = jnp.where(sub == j, adv_ref[j], wanted)
    owned = (wanted == m * 64 + lax.broadcasted_iota(jnp.int32, (8, 64), 1)).astype(F32).astype(BF16)
    for x in range(4):
        for row in range(2):
            ids = slab_ref[x, row : row + 1, :]
            vol = jnp.zeros((1, 128), F32)
            for level in range(8):
                vol = jnp.where(ids == level, vol_ref[level], vol)
            vol = vol * (0.5 * scale)
            for d in range(3):
                part[row * 4 + x, d] = vol * jnp.dot(owned, u_ref[row, d * 4 + x], preferred_element_type=F32)
    pl.semaphore_wait(barrier, jnp.where(stays, len(peers), len(peers) + 2))

    def piece(ref, p):
        return ref.at[p // 2, pl.ds((p % 2) * 6, 6)]

    def rs_copy(t):
        n = n_ring[t]
        return rcopy(part.at[n], rs_buf.at[m], rs_s.at[t], rs_r.at[m], place(core - z + vq, n))

    for t in range(1, 8):
        rs_copy(t).start()

    @pl.when(stays)
    def _():
        pltpu.make_async_copy(part.at[vm], rs_buf.at[m], rs_r.at[m]).start()
        for p in range(4):
            pltpu.make_async_copy(piece(u_ref, p), piece(ub, p), own_r.at[p]).start()

    def swap(p):
        return rcopy(piece(u_ref, p), piece(ub, p), own_s.at[p], own_r.at[p], dev(vq, vm))

    @pl.when(jnp.logical_not(stays))
    def _():
        rs_copy(0).start()
        for p in range(4):
            swap(p).start()

    up_y = place(vq, core * 4 + ynext)
    down_y = place(vq, core * 4 + yprev)
    to_core = place(vq, (1 - core) * 4 + y)

    def move(src, slot, p, target):
        return rcopy(piece(src, p), piece(blk.at[slot], p), bulk_s.at[slot * 4 + p], bulk_r.at[slot * 4 + p], target)

    started = []

    def go(src, slot, p, target):
        copy = move(src, slot, p, target)
        copy.start()
        started.append(copy)

    def arrived(slot, p):
        move(u_ref, slot, p, here).wait_recv()

    def start_own(p):
        swap(p).wait_recv()
        go(ub, 0, p, up_y)
        go(ub, 1, p, down_y)
        go(ub, 2, p, to_core)

    halo = [
        rcopy(u_ref.at[0], hal.at[1], halo_s.at[0], halo_r.at[0], place(qprev, m)),
        rcopy(u_ref.at[1], hal.at[0], halo_s.at[1], halo_r.at[1], place(qnext, m)),
    ]
    start_own(0)
    start_own(1)
    halo[0].start()
    halo[1].start()

    total = None
    for n in range(8):
        rcopy(part.at[n], rs_buf.at[n], rs_s.at[n], rs_r.at[n], here).wait_recv()
        total = rs_buf[n] if total is None else total + rs_buf[n]
    h_ref[vm] = total

    def ag_copy(t, block):
        return rcopy(h_ref.at[block], h_ref.at[block], ag_s.at[t], ag_r.at[block], place(vq, n_ring[t]))

    vside = jnp.where(core == 0, vprev, vnext)

    def hy_copy(t):
        return rcopy(
            h_ref.at[vm, 1], hyh.at[1 - core, y], hy_s.at[t], hy_r.at[(1 - core) * 4 + y], place(vside, n_ring[t])
        )

    for t in range(8):
        if t > 0:
            ag_copy(t, vm).start()
        hy_copy(t).start()
    start_own(2)
    start_own(3)

    def shift(k, carry):
        for row in range(2):
            tile = ub[row, k].astype(F32)
            up[row, k] = pltpu.roll(tile, 127, 1).astype(BF16)
            um[row, k] = pltpu.roll(tile, 1, 1).astype(BF16)
        return carry

    lax.fori_loop(0, 12, shift, 0)

    def pick_modes(k, carry):
        at = pl.ds(pl.multiple_of(k * 256, 256), 256)
        rows = lax.broadcasted_iota(jnp.int32, (512, 256), 0)
        onehot[:, at] = (rows == pmode_ref[:, at]).astype(F32).astype(BF16)
        return carry

    lax.fori_loop(0, 8, pick_modes, 0)
    mask[...] = (lax.broadcasted_iota(jnp.int32, (8, 2048), 0) == padv_ref[...]).astype(F32)

    for t in range(1, 8):
        ag_copy(t, n_ring[t]).wait_recv()
    for n in range(8):
        hzp[n] = pltpu.roll(h_ref[n, 2], 127, 1)
        hzm[n] = pltpu.roll(h_ref[n, 2], 1, 1)

    for p in (0, 1):
        arrived(0, p)
        go(blk.at[0], 5, p, up_y)
        go(blk.at[0], 3, p, to_core)
        arrived(1, p)
        go(blk.at[1], 4, p, to_core)
    for p in (2, 3):
        arrived(1, p)
        go(blk.at[1], 5, p, down_y)
        go(blk.at[1], 4, p, to_core)
        arrived(0, p)
        go(blk.at[0], 3, p, to_core)

    amp_copy.wait()

    def split_amp(k, carry):
        at = pl.ds(pl.multiple_of(k * 32, 32), 32)
        value = amp[at]
        hi = value.astype(BF16)
        amp_hi[at] = hi
        amp_lo[at] = (value - hi.astype(F32)).astype(BF16)
        return carry

    lax.fori_loop(0, 64, split_amp, 0)

    halo[0].wait_recv()
    halo[1].wait_recv()
    for i in range(2):
        for x in range(4):
            rcopy(hyh.at[i, x], hyh.at[i, x], hy_s.at[x], hy_r.at[i * 4 + x], here).wait_recv()

    first_ok = jnp.where(vq == 0, 0.0, 1.0)
    last_ok = jnp.where(vq == 31, 0.0, 1.0)

    def build(row, c, carry_in):
        def one(x, carry):
            xp = lax.rem(x + 1, 4)
            xm = lax.rem(x + 3, 4)
            at, atp, atm = c * 4 + x, c * 4 + xp, c * 4 + xm
            n = row * 4 + x
            for g in range(2):
                cut = pl.ds(g * 32, 32)
                uxp = ub[row, atp, cut].astype(F32)
                uxm = ub[row, atm, cut].astype(F32)
                uzp = up[row, at, cut].astype(F32)
                uzm = um[row, at, cut].astype(F32)
                if row == 0:
                    uyp = ub[1, at, cut].astype(F32)
                    uym = hal[0, at, cut].astype(F32) * first_ok
                else:
                    uyp = hal[1, at, cut].astype(F32) * last_ok
                    uym = ub[0, at, cut].astype(F32)
                for j in range(8):
                    js = slice(j, j + 1)
                    hyp = h_ref[4 + x, 1, js] if row == 0 else hyh[1, x, js]
                    hym = hyh[0, x, js] if row == 0 else h_ref[x, 1, js]
                    qq = h_ref[row * 4 + xm, 0, js] * uxm - h_ref[row * 4 + xp, 0, js] * uxp
                    qq = qq + (hym * uym - hyp * uyp)
                    qq = qq + (hzm[n, js] * uzm - hzp[n, js] * uzp)
                    lines = pl.ds(j * 64 + g * 32, 32)
                    q_ref[row, at, lines] = qq.astype(BF16)
            return carry

        return lax.fori_loop(0, 4, one, carry_in)

    for row in range(2):
        lax.fori_loop(0, 3, functools.partial(build, row), 0)
        for p in (2 * row, 2 * row + 1):
            arrived(5, p)
            go(blk.at[5], 6, p, to_core)

    def x_copy(n, t):
        return rcopy(
            tb.at[n, :, e_ring[t]], xbuf.at[n, e // 2 * 2 + z], x_s.at[n, t], x_r.at[n, e // 2 * 2 + z],
            dev(zh * 8 + e_ring[t], vm),
        )

    def send_batch(n):
        for k in range(2):
            tb[n, :, :, :, pl.ds(k * 128, 128)] = tf[k].astype(BF16).reshape(4, 8, 16, 128)

        @pl.when(stays)
        def _():
            slot = e // 2 * 2 + z
            pltpu.make_async_copy(tb.at[n, :, e], xbuf.at[n, slot], x_r.at[n, slot]).start()

        @pl.when(jnp.logical_not(stays))
        def _():
            x_copy(n, 0).start()

        for t in range(1, 8):
            x_copy(n, t).start()

    def products(n, parts):
        total = None
        for r in range(2):
            pair = jnp.concatenate(
                [jnp.concatenate([ref[r, k] for k in range(12)], axis=1) for ref in parts], axis=0
            )
            left = jnp.concatenate([q_ref[r, k] for k in range(12)], axis=1)
            value = lax.dot_general(left, pair, NT, preferred_element_type=F32)
            total = value if total is None else total + value
        for j in range(8):
            for k in range(2):
                tf[k, pl.ds(j, 64, stride=8), :] = total[j * 64 : (j + 1) * 64, k * 128 : (k + 1) * 128]
        send_batch(n)

    def z_copy(n, t):
        return rcopy(zsrc.at[n, lax.rem(zh + t, 4)], zbuf.at[n, t], z_s.at[n, t], z_r.at[n, t], dev(z_ring[t], m))

    def gather_batch(n):
        total = None
        for t in range(8):
            rcopy(xbuf.at[n, t], xbuf.at[n, t], x_s.at[n, t], x_r.at[n, t], here).wait_recv()
            value = xbuf[n, t].astype(F32)
            total = value if total is None else total + value
        zsrc[n] = total
        for t in range(1, 4):
            z_copy(n, t).start()

    for p in range(4):
        arrived(2, p)
    products(0, (ub, blk.at[2], blk.at[0], blk.at[1]))
    for p in range(4):
        arrived(3, p)
        arrived(4, p)
        arrived(6, p)
    products(1, (blk.at[3], blk.at[4], blk.at[5], blk.at[6]))
    gather_batch(0)
    gather_batch(1)

    blocks = [
        (m, (1 - z) * 4 + y, z * 4 + yprev, z * 4 + ynext),
        ((1 - z) * 4 + yprev, (1 - z) * 4 + ynext, z * 4 + yfar, (1 - z) * 4 + yfar),
    ]
    for n in range(2):
        value = zsrc[n, zh]
        for t in range(1, 4):
            z_copy(n, t).wait_recv()
            value = value + zbuf[n, t]
        for k in range(2):
            pair = value[:, k * 128 : (k + 1) * 128]
            fin[blocks[n][2 * k]] = pair
            fin[blocks[n][2 * k + 1]] = pltpu.roll(pair, 64, 1)

    low = lax.broadcasted_iota(jnp.int32, (16, 128), 1) < 64
    columns = []
    for t in range(4):
        columns.append(jnp.where(low, fin[2 * t], pltpu.roll(fin[2 * t + 1], 64, 1)))
    tensor = jnp.concatenate(columns, axis=1)
    out_ref[...] = tensor
    top = tensor.astype(BF16)
    rest = (tensor - top.astype(F32)).astype(BF16)
    chosen = jnp.dot(jnp.concatenate([top, rest], axis=0), onehot[...], preferred_element_type=F32)
    chosen = chosen[:16] + chosen[16:]
    first = jnp.sum(chosen[:8] * mask[...], axis=0, keepdims=True)
    second = jnp.sum(chosen[8:] * mask[...], axis=0, keepdims=True)
    rows = lax.broadcasted_iota(jnp.int32, (16, 2048), 0)
    both = jnp.where(lax.rem(rows, 2) == 0, first, second)
    both_hi = both.astype(BF16).astype(F32)
    stacked = jnp.where(rows < 2, both_hi, jnp.where(rows < 4, both - both_hi, 0.0)).astype(BF16)
    answer = jnp.dot(stacked, amp_hi[...], preferred_element_type=F32)
    answer = answer + jnp.dot(stacked, amp_lo[...], preferred_element_type=F32)
    resp_ref[...] = answer[0:2] + answer[2:4]

    for t in range(1, 8):
        rs_copy(t).wait_send()
        ag_copy(t, vm).wait_send()
    for t in range(8):
        hy_copy(t).wait_send()
    for copy in started + halo:
        copy.wait_send()
    for n in range(2):
        for t in range(1, 8):
            x_copy(n, t).wait_send()
        for t in range(1, 4):
            z_copy(n, t).wait_send()

    @pl.when(jnp.logical_not(stays))
    def _():
        rs_copy(0).wait_send()
        for p in range(4):
            swap(p).wait_send()
        for n in range(2):
            x_copy(n, 0).wait_send()


def finish(tensor_ref, response_ref, out_ref, resp_ref):
    out_ref[...] = tensor_ref[...]
    resp_ref[...] = response_ref[...]


def shards(pod_modes, slab_map, slab_volume, advect_index, pair_adv, pair_mode, pair_amp):
    cells = pod_modes.shape[2] * pod_modes.shape[3] * lax.axis_size("cell") * pod_modes.shape[4]
    u = jnp.transpose(pod_modes, (3, 0, 2, 1, 4)).reshape(2, 12, 64, 128)
    vmem = pl.BlockSpec(memory_space=pltpu.VMEM)
    smem = pl.BlockSpec(memory_space=pltpu.SMEM)
    dma = pltpu.SemaphoreType.DMA
    shapes = (jax.ShapeDtypeStruct((16, 512), F32), jax.ShapeDtypeStruct((2, 1024), F32))
    results = pl.pallas_call(
        functools.partial(kernel, float(cells) ** -0.5),
        out_shape=shapes,
        in_specs=[vmem, vmem, smem, smem, vmem, vmem, pl.BlockSpec(memory_space=pl.ANY)],
        out_specs=(vmem, vmem),
        scratch_shapes=[
            pltpu.VMEM((2, 12, 64, 128), BF16),
            pltpu.VMEM((7, 2, 12, 64, 128), BF16),
            pltpu.VMEM((2, 12, 64, 128), BF16),
            pltpu.VMEM((2, 12, 64, 128), BF16),
            pltpu.VMEM((2, 12, 64, 128), BF16),
            pltpu.VMEM((2, 12, 512, 128), BF16),
            pltpu.VMEM((8, 3, 8, 128), F32),
            pltpu.VMEM((8, 3, 8, 128), F32),
            pltpu.VMEM((8, 3, 8, 128), F32),
            pltpu.VMEM((2, 4, 8, 128), F32),
            pltpu.VMEM((8, 8, 128), F32),
            pltpu.VMEM((8, 8, 128), F32),
            pltpu.VMEM((2, 512, 128), F32),
            pltpu.VMEM((2, 4, 8, 16, 256), BF16),
            pltpu.VMEM((2, 8, 4, 16, 256), BF16),
            pltpu.VMEM((2, 4, 16, 256), F32),
            pltpu.VMEM((2, 4, 16, 256), F32),
            pltpu.VMEM((8, 16, 128), F32),
            pltpu.VMEM((2048, 1024), F32),
            pltpu.VMEM((2048, 1024), BF16),
            pltpu.VMEM((2048, 1024), BF16),
            pltpu.VMEM((512, 2048), BF16),
            pltpu.VMEM((8, 2048), F32),
            dma((8,)), dma((8,)), dma((8,)), dma((8,)),
            dma((4,)), dma((4,)), dma((28,)), dma((28,)), dma((2,)), dma((2,)), dma((8,)), dma((8,)),
            dma((2, 8)), dma((2, 8)), dma((2, 4)), dma((2, 4)), dma,
        ],
        compiler_params=pltpu.CompilerParams(
            collective_id=0, has_side_effects=True, vmem_limit_bytes=60 * 2**20
        ),
        name="pod_tensor",
    )(
        u, slab_map, slab_volume, advect_index,
        pair_adv.reshape(1, -1), pair_mode.reshape(1, -1), pair_amp,
    )
    tensor, response = pl.pallas_call(
        finish, out_shape=shapes, in_specs=[vmem, vmem], out_specs=(vmem, vmem), name="finish"
    )(*results)
    return tensor.reshape(2, 8, 512), response


def solution(mesh):
    in_specs = (P(None, "mode", None, "cell", None), P(None, "cell", None), P(), P(), P(), P(), P())
    out_specs = (P(("mode", "cell"), None, None), P(("mode", "cell"), None))
    return jax.shard_map(shards, mesh=mesh, in_specs=in_specs, out_specs=out_specs, check_vma=False)
```

time: 66.8 us -> 56.5 us (0.85)
  Pallas kernels: 61.3 us -> 53.8 us
  local copies, waits for them, and re-layouts: 4.65 us -> 1.83 us
    pallas_call x1, Pallas kernels: 61.3 us -> 52.4 us  [shards(): pl.pallas_call(functools.partial(kernel, float(cells) ** (-0.5)), out_sha...]
    unnamed x2 -> x0, local copies, waits for them, and re-layouts: 2.67 us -> none
    pallas_call x0 -> x1, Pallas kernels: none -> 1.38 us  [shards(): pl.pallas_call(finish, out_shape=shapes, in_specs=[vmem, vmem], out_specs...]
    reshape x1 -> x0, local copies, waits for them, and re-layouts: 0.88 us -> none  [shards(): u = jnp.transpose(pod_modes, (3, 1, 0, 2, 4)).reshape(2, 64, 1536)]
    transpose x1, local copies, waits for them, and re-layouts: 1.1 us -> 1.83 us  [shards(): u = jnp.transpose(pod_modes, (3, 0, 2, 1, 4)).reshape(2, 12, 64, 128)]
where the time goes in v2:
time: 56.5 us; the launch traced here: 56.3 us
  Pallas kernels  53.8 us (95%)
  local copies, waits for them, and re-layouts  1.83 us (3%)
  between operations  0.64 us (1%)
    pallas_call x1, Pallas kernels, shards(): pl.pallas_call(functools.partial(kernel, float(cells) ** (-0.5)), out_sha...  52.4 us
    transpose x1, local copies, waits for them, and re-layouts, shards(): u = jnp.transpose(pod_modes, (3, 0, 2, 1, 4)).reshape(2, 12, 64, 128)  1.83 us
    pallas_call x1, Pallas kernels, shards(): pl.pallas_call(finish, out_shape=shapes, in_specs=[vmem, vmem], out_specs...  1.38 us

profile of v2, /device:TPU:1, one launch (start us, length us, event | category | flops | bytes accessed | tf_op | source)
XLA Modules:
  0.0 56.3 jit_solution(15952223508147749303)
XLA Ops:
  0.6 1.8 %copy.9 = bf16[2,3,4,64,128]{4,3,2,1,0:T(8,128)(2,1)} copy(bf16[2,3,4,64,128]{4,0,2,3,1:T(2,128)(2,1)} %bitcast.6) | data formatting | bytes 786432 | tf_op jit(solution)/shard_map/transpose | solution.py:398
  2.5 52.4 %pod_tensor.1 = (f32[16,512]{1,0:T(8,128)}, f32[2,1024]{1,0:T(2,128)}) custom-call(bf16[2,12,64,128]{3,2,1,0:T(8,128)(2,1)} %bitcast.5, s32[4,2,128]{2,1,0:T(2,128)} %slab_ref.1, f32[8]{0:T(128)} %vol_ref.1, s32[8]{0:T(128)} %adv_ref.1, s32[1,2048]{1,0:T(1,128)} %bitcast.7, s32[1,2048]{1,0:T(1,128)} %bitcast.8, f32[2048,1024]{1,0:T(8,128)} %amp_hbm.1), custom_call_target="tpu_custom_call" | custom-call | tf_op jit(solution)/shard_map/pod_tensor/pallas_call | solution.py:403
  54.9 1.4 %finish.1 = (f32[16,512]{1,0:T(8,128)}, f32[2,1024]{1,0:T(2,128)}) custom-call(f32[16,512]{1,0:T(8,128)} %get-tuple-element.6.tensor_ref, f32[2,1024]{1,0:T(2,128)} %get-tuple-element.7.response_ref), custom_call_target="tpu_custom_call" | custom-call | tf_op jit(solution)/shard_map/finish/pallas_call | solution.py:444

commit v3 on v2

--- a/solution.py
+++ b/solution.py
@@ -20,7 +20,7 @@
     part, rs_buf, h_ref, hyh, hzp, hzm,
     tf, tb, xbuf, zsrc, zbuf, fin,
     amp, amp_hi, amp_lo, onehot, mask,
-    rs_s, rs_r, ag_s, ag_r, own_s, own_r, bulk_s, bulk_r, halo_s, halo_r, hy_s, hy_r, x_s, x_r, z_s, z_r, amp_sem,
+    rs_s, rs_r, ag_s, ag_r, own_s, own_r, bulk_s, bulk_r, halo_s, halo_r, hy_s, hy_r, x_s, x_r, z_s, z_r, amp_sem, token,
 ):
     q = lax.axis_index("cell")
     m = lax.axis_index("mode")
@@ -29,6 +29,7 @@
     zh = q // 8
     z = m // 4
     y = lax.rem(m, 4)
+    zb = 1 - z
     stays = core == z
     vq = q - core + z
     vm = core * 4 + y
@@ -58,13 +59,15 @@
     qnext = lax.rem(q + 1, 32)
 
     barrier = pltpu.get_barrier_semaphore()
+    z_up = dev(lax.rem(zh + z, 4) * 8 + e, zb * 4 + y)
+    z_down = dev(lax.rem(zh + 3 + z, 4) * 8 + e, zb * 4 + y)
     y_of = [lax.rem(y + t, 4) for t in range(4)]
     peers = [place(vq, n_ring[t]) for t in range(1, 8)]
     peers += [dev(vq, lax.rem(z + t // 4, 2) * 4 + y_of[t % 4]) for t in range(1, 8)]
     peers += [
         dev(zh * 8 + lax.rem(e // 2 + t // 2, 4) * 2 + z, lax.rem(z + t, 2) * 4 + y) for t in range(1, 8)
     ]
-    peers += [dev(z_ring[t], m) for t in range(1, 4)]
+    peers += [z_up, z_down]
     peers += [dev(vprev, vm), dev(vnext, vm)]
     peers += [place(vnext, x) for x in range(4)] + [place(vprev, 4 + x) for x in range(4)]
 
@@ -100,6 +103,16 @@
     def piece(ref, p):
         return ref.at[p // 2, pl.ds((p % 2) * 6, 6)]
 
+    def pass_token(k):
+        pl.semaphore_signal(token.at[k, 0], inc=1, device_id=z_up, device_id_type=MESH)
+        pl.semaphore_signal(token.at[k, 1], inc=1, device_id=z_down, device_id_type=MESH)
+
+    def take_token(k):
+        pl.semaphore_wait(token.at[k, 0], 1)
+        pl.semaphore_wait(token.at[k, 1], 1)
+
+    pass_token(0)
+
     def rs_copy(t):
         n = n_ring[t]
         return rcopy(part.at[n], rs_buf.at[m], rs_s.at[t], rs_r.at[m], place(core - z + vq, n))
@@ -119,7 +132,7 @@
     @pl.when(jnp.logical_not(stays))
     def _():
         rs_copy(0).start()
-        for p in range(4):
+        for p in (0, 2, 1, 3):
             swap(p).start()
 
     up_y = place(vq, core * 4 + ynext)
@@ -139,26 +152,34 @@
     def arrived(slot, p):
         move(u_ref, slot, p, here).wait_recv()
 
-    def start_own(p):
+    def start_first(p):
         swap(p).wait_recv()
         go(ub, 0, p, up_y)
+        swap(p + 2).wait_recv()
+        go(ub, 1, p + 2, down_y)
+
+    def start_rest(p):
+        go(ub, 0, p + 2, up_y)
         go(ub, 1, p, down_y)
         go(ub, 2, p, to_core)
+        go(ub, 2, p + 2, to_core)
 
     halo = [
         rcopy(u_ref.at[0], hal.at[1], halo_s.at[0], halo_r.at[0], place(qprev, m)),
         rcopy(u_ref.at[1], hal.at[0], halo_s.at[1], halo_r.at[1], place(qnext, m)),
     ]
-    start_own(0)
-    start_own(1)
-    halo[0].start()
-    halo[1].start()
+    for p in range(2):
+        start_first(p)
+    for p in range(2):
+        start_rest(p)
 
     total = None
     for n in range(8):
         rcopy(part.at[n], rs_buf.at[n], rs_s.at[n], rs_r.at[n], here).wait_recv()
         total = rs_buf[n] if total is None else total + rs_buf[n]
     h_ref[vm] = total
+    take_token(0)
+    pass_token(1)
 
     def ag_copy(t, block):
         return rcopy(h_ref.at[block], h_ref.at[block], ag_s.at[t], ag_r.at[block], place(vq, n_ring[t]))
@@ -174,8 +195,16 @@
         if t > 0:
             ag_copy(t, vm).start()
         hy_copy(t).start()
-    start_own(2)
-    start_own(3)
+    halo[0].start()
+    halo[1].start()
+
+    for p in range(2):
+        arrived(0, p)
+        go(blk.at[0], 5, p, up_y)
+        go(blk.at[0], 3, p, to_core)
+        arrived(1, p + 2)
+        go(blk.at[1], 5, p + 2, down_y)
+        go(blk.at[1], 4, p + 2, to_core)
 
     def shift(k, carry):
         for row in range(2):
@@ -186,45 +215,19 @@
 
     lax.fori_loop(0, 12, shift, 0)
 
-    def pick_modes(k, carry):
-        at = pl.ds(pl.multiple_of(k * 256, 256), 256)
-        rows = lax.broadcasted_iota(jnp.int32, (512, 256), 0)
-        onehot[:, at] = (rows == pmode_ref[:, at]).astype(F32).astype(BF16)
-        return carry
-
-    lax.fori_loop(0, 8, pick_modes, 0)
-    mask[...] = (lax.broadcasted_iota(jnp.int32, (8, 2048), 0) == padv_ref[...]).astype(F32)
-
     for t in range(1, 8):
         ag_copy(t, n_ring[t]).wait_recv()
+    take_token(1)
+    pass_token(2)
     for n in range(8):
         hzp[n] = pltpu.roll(h_ref[n, 2], 127, 1)
         hzm[n] = pltpu.roll(h_ref[n, 2], 1, 1)
 
-    for p in (0, 1):
-        arrived(0, p)
-        go(blk.at[0], 5, p, up_y)
-        go(blk.at[0], 3, p, to_core)
+    for p in range(2):
+        arrived(0, p + 2)
+        go(blk.at[0], 3, p + 2, to_core)
         arrived(1, p)
         go(blk.at[1], 4, p, to_core)
-    for p in (2, 3):
-        arrived(1, p)
-        go(blk.at[1], 5, p, down_y)
-        go(blk.at[1], 4, p, to_core)
-        arrived(0, p)
-        go(blk.at[0], 3, p, to_core)
-
-    amp_copy.wait()
-
-    def split_amp(k, carry):
-        at = pl.ds(pl.multiple_of(k * 32, 32), 32)
-        value = amp[at]
-        hi = value.astype(BF16)
-        amp_hi[at] = hi
-        amp_lo[at] = (value - hi.astype(F32)).astype(BF16)
-        return carry
-
-    lax.fori_loop(0, 64, split_amp, 0)
 
     halo[0].wait_recv()
     halo[1].wait_recv()
@@ -268,9 +271,6 @@
 
     for row in range(2):
         lax.fori_loop(0, 3, functools.partial(build, row), 0)
-        for p in (2 * row, 2 * row + 1):
-            arrived(5, p)
-            go(blk.at[5], 6, p, to_core)
 
     def x_copy(n, t):
         return rcopy(
@@ -279,8 +279,7 @@
         )
 
     def send_batch(n):
-        for k in range(2):
-            tb[n, :, :, :, pl.ds(k * 128, 128)] = tf[k].astype(BF16).reshape(4, 8, 16, 128)
+        tb[n] = tf[n].astype(BF16).reshape(4, 8, 16, 128)
 
         @pl.when(stays)
         def _():
@@ -294,7 +293,7 @@
         for t in range(1, 8):
             x_copy(n, t).start()
 
-    def products(n, parts):
+    def products(first, parts):
         total = None
         for r in range(2):
             pair = jnp.concatenate(
@@ -303,10 +302,10 @@
             left = jnp.concatenate([q_ref[r, k] for k in range(12)], axis=1)
             value = lax.dot_general(left, pair, NT, preferred_element_type=F32)
             total = value if total is None else total + value
-        for j in range(8):
-            for k in range(2):
-                tf[k, pl.ds(j, 64, stride=8), :] = total[j * 64 : (j + 1) * 64, k * 128 : (k + 1) * 128]
-        send_batch(n)
+        for k in range(len(parts) // 2):
+            for j in range(8):
+                tf[first + k, pl.ds(j, 64, stride=8), :] = total[j * 64 : (j + 1) * 64, k * 128 : (k + 1) * 128]
+            send_batch(first + k)
 
     def z_copy(n, t):
         return rcopy(zsrc.at[n, lax.rem(zh + t, 4)], zbuf.at[n, t], z_s.at[n, t], z_r.at[n, t], dev(z_ring[t], m))
@@ -323,28 +322,65 @@
 
     for p in range(4):
         arrived(2, p)
+    for p in (0, 2, 1, 3):
+        arrived(5, p)
+        go(blk.at[5], 6, p, to_core)
     products(0, (ub, blk.at[2], blk.at[0], blk.at[1]))
     for p in range(4):
         arrived(3, p)
         arrived(4, p)
+    products(2, (blk.at[3], blk.at[4]))
+    for p in range(4):
         arrived(6, p)
-    products(1, (blk.at[3], blk.at[4], blk.at[5], blk.at[6]))
-    gather_batch(0)
-    gather_batch(1)
+    products(3, (blk.at[5], blk.at[6]))
+    def pick_modes(k, carry):
+        at = pl.ds(pl.multiple_of(k * 256, 256), 256)
+        rows = lax.broadcasted_iota(jnp.int32, (512, 256), 0)
+        onehot[:, at] = (rows == pmode_ref[:, at]).astype(F32).astype(BF16)
+        return carry
+
+    lax.fori_loop(0, 8, pick_modes, 0)
+    mask[...] = (lax.broadcasted_iota(jnp.int32, (8, 2048), 0) == padv_ref[...]).astype(F32)
+
+    amp_copy.wait()
+
+    def split_amp(k, carry):
+        at = pl.ds(pl.multiple_of(k * 32, 32), 32)
+        value = amp[at]
+        hi = value.astype(BF16)
+        amp_hi[at] = hi
+        amp_lo[at] = (value - hi.astype(F32)).astype(BF16)
+        return carry
+
+    lax.fori_loop(0, 64, split_amp, 0)
+
+    for t in range(1, 8):
+        rs_copy(t).wait_send()
+        ag_copy(t, vm).wait_send()
+    for t in range(8):
+        hy_copy(t).wait_send()
+    for copy in started + halo:
+        copy.wait_send()
+    take_token(2)
+    for n in range(4):
+        gather_batch(n)
+    for n in range(4):
+        for t in range(1, 8):
+            x_copy(n, t).wait_send()
 
     blocks = [
-        (m, (1 - z) * 4 + y, z * 4 + yprev, z * 4 + ynext),
-        ((1 - z) * 4 + yprev, (1 - z) * 4 + ynext, z * 4 + yfar, (1 - z) * 4 + yfar),
+        (m, zb * 4 + y),
+        (z * 4 + yprev, z * 4 + ynext),
+        (zb * 4 + yprev, zb * 4 + ynext),
+        (z * 4 + yfar, zb * 4 + yfar),
     ]
-    for n in range(2):
+    for n in range(4):
         value = zsrc[n, zh]
         for t in range(1, 4):
             z_copy(n, t).wait_recv()
             value = value + zbuf[n, t]
-        for k in range(2):
-            pair = value[:, k * 128 : (k + 1) * 128]
-            fin[blocks[n][2 * k]] = pair
-            fin[blocks[n][2 * k + 1]] = pltpu.roll(pair, 64, 1)
+        fin[blocks[n][0]] = value
+        fin[blocks[n][1]] = pltpu.roll(value, 64, 1)
 
     low = lax.broadcasted_iota(jnp.int32, (16, 128), 1) < 64
     columns = []
@@ -366,16 +402,7 @@
     answer = answer + jnp.dot(stacked, amp_lo[...], preferred_element_type=F32)
     resp_ref[...] = answer[0:2] + answer[2:4]
 
-    for t in range(1, 8):
-        rs_copy(t).wait_send()
-        ag_copy(t, vm).wait_send()
-    for t in range(8):
-        hy_copy(t).wait_send()
-    for copy in started + halo:
-        copy.wait_send()
-    for n in range(2):
-        for t in range(1, 8):
-            x_copy(n, t).wait_send()
+    for n in range(4):
         for t in range(1, 4):
             z_copy(n, t).wait_send()
 
@@ -384,7 +411,7 @@
         rs_copy(0).wait_send()
         for p in range(4):
             swap(p).wait_send()
-        for n in range(2):
+        for n in range(4):
             x_copy(n, 0).wait_send()
 
 
@@ -418,11 +445,11 @@
             pltpu.VMEM((2, 4, 8, 128), F32),
             pltpu.VMEM((8, 8, 128), F32),
             pltpu.VMEM((8, 8, 128), F32),
-            pltpu.VMEM((2, 512, 128), F32),
-            pltpu.VMEM((2, 4, 8, 16, 256), BF16),
-            pltpu.VMEM((2, 8, 4, 16, 256), BF16),
-            pltpu.VMEM((2, 4, 16, 256), F32),
-            pltpu.VMEM((2, 4, 16, 256), F32),
+            pltpu.VMEM((4, 512, 128), F32),
+            pltpu.VMEM((4, 4, 8, 16, 128), BF16),
+            pltpu.VMEM((4, 8, 4, 16, 128), BF16),
+            pltpu.VMEM((4, 4, 16, 128), F32),
+            pltpu.VMEM((4, 4, 16, 128), F32),
             pltpu.VMEM((8, 16, 128), F32),
             pltpu.VMEM((2048, 1024), F32),
             pltpu.VMEM((2048, 1024), BF16),
@@ -431,7 +458,8 @@
             pltpu.VMEM((8, 2048), F32),
             dma((8,)), dma((8,)), dma((8,)), dma((8,)),
             dma((4,)), dma((4,)), dma((28,)), dma((28,)), dma((2,)), dma((2,)), dma((8,)), dma((8,)),
-            dma((2, 8)), dma((2, 8)), dma((2, 4)), dma((2, 4)), dma,
+            dma((4, 8)), dma((4, 8)), dma((4, 4)), dma((4, 4)), dma,
+            pltpu.SemaphoreType.REGULAR((3, 2)),
         ],
         compiler_params=pltpu.CompilerParams(
             collective_id=0, has_side_effects=True, vmem_limit_bytes=60 * 2**20

time: 56.5 us -> 54.4 us (0.963)
  Pallas kernels: 53.8 us -> 51.7 us
    pallas_call x1, Pallas kernels: 52.4 us -> 50.3 us  [shards(): pl.pallas_call(functools.partial(kernel, float(cells) ** (-0.5)), out_sha...]
where the time goes in v3:
time: 54.4 us; the launch traced here: 54.2 us
  Pallas kernels  51.7 us (95%)
  local copies, waits for them, and re-layouts  1.83 us (3%)
  between operations  0.64 us (1%)
    pallas_call x1, Pallas kernels, shards(): pl.pallas_call(functools.partial(kernel, float(cells) ** (-0.5)), out_sha...  50.3 us
    transpose x1, local copies, waits for them, and re-layouts, shards(): u = jnp.transpose(pod_modes, (3, 0, 2, 1, 4)).reshape(2, 12, 64, 128)  1.83 us
    pallas_call x1, Pallas kernels, shards(): pl.pallas_call(finish, out_shape=shapes, in_specs=[vmem, vmem], out_specs...  1.38 us

profile of v3, /device:TPU:1, one launch (start us, length us, event | category | flops | bytes accessed | tf_op | source)
XLA Modules:
  0.0 54.2 jit_solution(15620259206144553428)
XLA Ops:
  0.6 1.8 %copy.9 = bf16[2,3,4,64,128]{4,3,2,1,0:T(8,128)(2,1)} copy(bf16[2,3,4,64,128]{4,0,2,3,1:T(2,128)(2,1)} %bitcast.6) | data formatting | bytes 786432 | tf_op jit(solution)/shard_map/transpose | solution.py:425
  2.5 50.3 %pod_tensor.1 = (f32[16,512]{1,0:T(8,128)}, f32[2,1024]{1,0:T(2,128)}) custom-call(bf16[2,12,64,128]{3,2,1,0:T(8,128)(2,1)} %bitcast.5, s32[4,2,128]{2,1,0:T(2,128)} %slab_ref.1, f32[8]{0:T(128)} %vol_ref.1, s32[8]{0:T(128)} %adv_ref.1, s32[1,2048]{1,0:T(1,128)} %bitcast.7, s32[1,2048]{1,0:T(1,128)} %bitcast.8, f32[2048,1024]{1,0:T(8,128)} %amp_hbm.1), custom_call_target="tpu_custom_call" | custom-call | tf_op jit(solution)/shard_map/pod_tensor/pallas_call | solution.py:430
  52.8 1.4 %finish.1 = (f32[16,512]{1,0:T(8,128)}, f32[2,1024]{1,0:T(2,128)}) custom-call(f32[16,512]{1,0:T(8,128)} %get-tuple-element.6.tensor_ref, f32[2,1024]{1,0:T(2,128)} %get-tuple-element.7.response_ref), custom_call_target="tpu_custom_call" | custom-call | tf_op jit(solution)/shard_map/finish/pallas_call | solution.py:472

commit v4 on v3

--- a/solution.py
+++ b/solution.py
@@ -238,74 +238,89 @@
     first_ok = jnp.where(vq == 0, 0.0, 1.0)
     last_ok = jnp.where(vq == 31, 0.0, 1.0)
 
-    def build(row, c, carry_in):
+    def build(g, row, c, carry_in):
         def one(x, carry):
             xp = lax.rem(x + 1, 4)
             xm = lax.rem(x + 3, 4)
             at, atp, atm = c * 4 + x, c * 4 + xp, c * 4 + xm
             n = row * 4 + x
-            for g in range(2):
-                cut = pl.ds(g * 32, 32)
-                uxp = ub[row, atp, cut].astype(F32)
-                uxm = ub[row, atm, cut].astype(F32)
-                uzp = up[row, at, cut].astype(F32)
-                uzm = um[row, at, cut].astype(F32)
-                if row == 0:
-                    uyp = ub[1, at, cut].astype(F32)
-                    uym = hal[0, at, cut].astype(F32) * first_ok
-                else:
-                    uyp = hal[1, at, cut].astype(F32) * last_ok
-                    uym = ub[0, at, cut].astype(F32)
-                for j in range(8):
-                    js = slice(j, j + 1)
-                    hyp = h_ref[4 + x, 1, js] if row == 0 else hyh[1, x, js]
-                    hym = hyh[0, x, js] if row == 0 else h_ref[x, 1, js]
-                    qq = h_ref[row * 4 + xm, 0, js] * uxm - h_ref[row * 4 + xp, 0, js] * uxp
-                    qq = qq + (hym * uym - hyp * uyp)
-                    qq = qq + (hzm[n, js] * uzm - hzp[n, js] * uzp)
-                    lines = pl.ds(j * 64 + g * 32, 32)
-                    q_ref[row, at, lines] = qq.astype(BF16)
+            cut = pl.ds(g * 32, 32)
+            uxp = ub[row, atp, cut].astype(F32)
+            uxm = ub[row, atm, cut].astype(F32)
+            uzp = up[row, at, cut].astype(F32)
+            uzm = um[row, at, cut].astype(F32)
+            if row == 0:
+                uyp = ub[1, at, cut].astype(F32)
+                uym = hal[0, at, cut].astype(F32) * first_ok
+            else:
+                uyp = hal[1, at, cut].astype(F32) * last_ok
+                uym = ub[0, at, cut].astype(F32)
+            for j in range(8):
+                js = slice(j, j + 1)
+                hyp = h_ref[4 + x, 1, js] if row == 0 else hyh[1, x, js]
+                hym = hyh[0, x, js] if row == 0 else h_ref[x, 1, js]
+                qq = h_ref[row * 4 + xm, 0, js] * uxm - h_ref[row * 4 + xp, 0, js] * uxp
+                qq = qq + (hym * uym - hyp * uyp)
+                qq = qq + (hzm[n, js] * uzm - hzp[n, js] * uzp)
+                lines = pl.ds(g * 256 + j * 32, 32)
+                q_ref[row, at, lines] = qq.astype(BF16)
             return carry
 
         return lax.fori_loop(0, 4, one, carry_in)
 
-    for row in range(2):
-        lax.fori_loop(0, 3, functools.partial(build, row), 0)
-
-    def x_copy(n, t):
+    def build_half(g):
+        for row in range(2):
+            lax.fori_loop(0, 3, functools.partial(build, g, row), 0)
+
+
+    spans = [((0, 2), (2, 2)), ((0, 2), (2, 2)), ((0, 4),), ((0, 4),)]
+    x_slot = e // 2 * 2 + z
+
+    def x_copy(n, s, t):
+        span = pl.ds(*spans[n][s])
         return rcopy(
-            tb.at[n, :, e_ring[t]], xbuf.at[n, e // 2 * 2 + z], x_s.at[n, t], x_r.at[n, e // 2 * 2 + z],
+            tb.at[n, span, e_ring[t]], xbuf.at[n, x_slot, span], x_s.at[n * 2 + s, t], x_r.at[n * 2 + s, x_slot],
             dev(zh * 8 + e_ring[t], vm),
         )
 
-    def send_batch(n):
-        tb[n] = tf[n].astype(BF16).reshape(4, 8, 16, 128)
+    def send_rows(n, s):
+        start, count = spans[n][s]
+        span = pl.ds(start, count)
+        tb[n, span] = tf[n, pl.ds(start * 128, count * 128)].astype(BF16).reshape(count, 8, 16, 128)
 
         @pl.when(stays)
         def _():
-            slot = e // 2 * 2 + z
-            pltpu.make_async_copy(tb.at[n, :, e], xbuf.at[n, slot], x_r.at[n, slot]).start()
+            pltpu.make_async_copy(
+                tb.at[n, span, e], xbuf.at[n, x_slot, span], x_r.at[n * 2 + s, x_slot]
+            ).start()
 
         @pl.when(jnp.logical_not(stays))
         def _():
-            x_copy(n, 0).start()
+            x_copy(n, s, 0).start()
 
         for t in range(1, 8):
-            x_copy(n, t).start()
-
-    def products(first, parts):
+            x_copy(n, s, t).start()
+
+    def products(first, s, parts):
+        start, count = spans[first][s]
         total = None
         for r in range(2):
             pair = jnp.concatenate(
                 [jnp.concatenate([ref[r, k] for k in range(12)], axis=1) for ref in parts], axis=0
             )
-            left = jnp.concatenate([q_ref[r, k] for k in range(12)], axis=1)
+            left = jnp.concatenate(
+                [q_ref[r, k, pl.ds(start * 128, count * 128)] for k in range(12)], axis=1
+            )
             value = lax.dot_general(left, pair, NT, preferred_element_type=F32)
             total = value if total is None else total + value
         for k in range(len(parts) // 2):
-            for j in range(8):
-                tf[first + k, pl.ds(j, 64, stride=8), :] = total[j * 64 : (j + 1) * 64, k * 128 : (k + 1) * 128]
-            send_batch(first + k)
+            for g in range(count // 2):
+                for j in range(8):
+                    rows = slice(g * 256 + j * 32, g * 256 + j * 32 + 32)
+                    tf[first + k, pl.ds(start * 128 + g * 256 + j, 32, stride=8), :] = total[
+                        rows, k * 128 : (k + 1) * 128
+                    ]
+            send_rows(first + k, s)
 
     def z_copy(n, t):
         return rcopy(zsrc.at[n, lax.rem(zh + t, 4)], zbuf.at[n, t], z_s.at[n, t], z_r.at[n, t], dev(z_ring[t], m))
@@ -313,7 +328,9 @@
     def gather_batch(n):
         total = None
         for t in range(8):
-            rcopy(xbuf.at[n, t], xbuf.at[n, t], x_s.at[n, t], x_r.at[n, t], here).wait_recv()
+            for s in range(len(spans[n])):
+                landed = xbuf.at[n, t, pl.ds(*spans[n][s])]
+                rcopy(landed, landed, x_s.at[n * 2 + s, t], x_r.at[n * 2 + s, t], here).wait_recv()
             value = xbuf[n, t].astype(F32)
             total = value if total is None else total + value
         zsrc[n] = total
@@ -322,17 +339,21 @@
 
     for p in range(4):
         arrived(2, p)
+    build_half(0)
+    near = (ub, blk.at[2], blk.at[0], blk.at[1])
+    products(0, 0, near)
+    build_half(1)
+    products(0, 1, near)
     for p in (0, 2, 1, 3):
         arrived(5, p)
         go(blk.at[5], 6, p, to_core)
-    products(0, (ub, blk.at[2], blk.at[0], blk.at[1]))
     for p in range(4):
         arrived(3, p)
         arrived(4, p)
-    products(2, (blk.at[3], blk.at[4]))
+    products(2, 0, (blk.at[3], blk.at[4]))
     for p in range(4):
         arrived(6, p)
-    products(3, (blk.at[5], blk.at[6]))
+    products(3, 0, (blk.at[5], blk.at[6]))
     def pick_modes(k, carry):
         at = pl.ds(pl.multiple_of(k * 256, 256), 256)
         rows = lax.broadcasted_iota(jnp.int32, (512, 256), 0)
@@ -366,7 +387,8 @@
         gather_batch(n)
     for n in range(4):
         for t in range(1, 8):
-            x_copy(n, t).wait_send()
+            for s in range(len(spans[n])):
+                x_copy(n, s, t).wait_send()
 
     blocks = [
         (m, zb * 4 + y),
@@ -412,7 +434,8 @@
         for p in range(4):
             swap(p).wait_send()
         for n in range(4):
-            x_copy(n, 0).wait_send()
+            for s in range(len(spans[n])):
+                x_copy(n, s, 0).wait_send()
 
 
 def finish(tensor_ref, response_ref, out_ref, resp_ref):
@@ -458,7 +481,7 @@
             pltpu.VMEM((8, 2048), F32),
             dma((8,)), dma((8,)), dma((8,)), dma((8,)),
             dma((4,)), dma((4,)), dma((28,)), dma((28,)), dma((2,)), dma((2,)), dma((8,)), dma((8,)),
-            dma((4, 8)), dma((4, 8)), dma((4, 4)), dma((4, 4)), dma,
+            dma((8, 8)), dma((8, 8)), dma((4, 4)), dma((4, 4)), dma,
             pltpu.SemaphoreType.REGULAR((3, 2)),
         ],
         compiler_params=pltpu.CompilerParams(

time: 54.4 us -> 53.9 us (level)
  no operation moved by 1% of the time
where the time goes in v4:
time: 53.9 us; the launch traced here: 53.7 us
  Pallas kernels  51.2 us (95%)
  local copies, waits for them, and re-layouts  1.83 us (3%)
  between operations  0.64 us (1%)
    pallas_call x1, Pallas kernels, shards(): pl.pallas_call(functools.partial(kernel, float(cells) ** (-0.5)), out_sha...  49.8 us
    transpose x1, local copies, waits for them, and re-layouts, shards(): u = jnp.transpose(pod_modes, (3, 0, 2, 1, 4)).reshape(2, 12, 64, 128)  1.83 us
    pallas_call x1, Pallas kernels, shards(): pl.pallas_call(finish, out_shape=shapes, in_specs=[vmem, vmem], out_specs...  1.38 us

profile of v4, /device:TPU:1, one launch (start us, length us, event | category | flops | bytes accessed | tf_op | source)
XLA Modules:
  0.0 53.7 jit_solution(2415160792542299137)
XLA Ops:
  0.6 1.8 %copy.9 = bf16[2,3,4,64,128]{4,3,2,1,0:T(8,128)(2,1)} copy(bf16[2,3,4,64,128]{4,0,2,3,1:T(2,128)(2,1)} %bitcast.6) | data formatting | bytes 786432 | tf_op jit(solution)/shard_map/transpose | solution.py:448
  2.5 49.8 %pod_tensor.1 = (f32[16,512]{1,0:T(8,128)}, f32[2,1024]{1,0:T(2,128)}) custom-call(bf16[2,12,64,128]{3,2,1,0:T(8,128)(2,1)} %bitcast.5, s32[4,2,128]{2,1,0:T(2,128)} %slab_ref.1, f32[8]{0:T(128)} %vol_ref.1, s32[8]{0:T(128)} %adv_ref.1, s32[1,2048]{1,0:T(1,128)} %bitcast.7, s32[1,2048]{1,0:T(1,128)} %bitcast.8, f32[2048,1024]{1,0:T(8,128)} %amp_hbm.1), custom_call_target="tpu_custom_call" | custom-call | tf_op jit(solution)/shard_map/pod_tensor/pallas_call | solution.py:453
  52.3 1.4 %finish.1 = (f32[16,512]{1,0:T(8,128)}, f32[2,1024]{1,0:T(2,128)}) custom-call(f32[16,512]{1,0:T(8,128)} %get-tuple-element.6.tensor_ref, f32[2,1024]{1,0:T(2,128)} %get-tuple-element.7.response_ref), custom_call_target="tpu_custom_call" | custom-call | tf_op jit(solution)/shard_map/finish/pallas_call | solution.py:495

commit v5 on v4

--- a/solution.py
+++ b/solution.py
@@ -342,11 +342,11 @@
     build_half(0)
     near = (ub, blk.at[2], blk.at[0], blk.at[1])
     products(0, 0, near)
-    build_half(1)
-    products(0, 1, near)
     for p in (0, 2, 1, 3):
         arrived(5, p)
         go(blk.at[5], 6, p, to_core)
+    build_half(1)
+    products(0, 1, near)
     for p in range(4):
         arrived(3, p)
         arrived(4, p)

time: 53.9 us -> 53.9 us (level)
  no operation moved by 1% of the time
where the time goes in v5:
time: 53.9 us; the launch traced here: 53.7 us
  Pallas kernels  51.2 us (95%)
  local copies, waits for them, and re-layouts  1.83 us (3%)
  between operations  0.64 us (1%)
    pallas_call x1, Pallas kernels, shards(): pl.pallas_call(functools.partial(kernel, float(cells) ** (-0.5)), out_sha...  49.8 us
    transpose x1, local copies, waits for them, and re-layouts, shards(): u = jnp.transpose(pod_modes, (3, 0, 2, 1, 4)).reshape(2, 12, 64, 128)  1.83 us
    pallas_call x1, Pallas kernels, shards(): pl.pallas_call(finish, out_shape=shapes, in_specs=[vmem, vmem], out_specs...  1.38 us

profile of v5, /device:TPU:1, one launch (start us, length us, event | category | flops | bytes accessed | tf_op | source)
XLA Modules:
  0.0 53.7 jit_solution(2811071949521165715)
XLA Ops:
  0.6 1.8 %copy.9 = bf16[2,3,4,64,128]{4,3,2,1,0:T(8,128)(2,1)} copy(bf16[2,3,4,64,128]{4,0,2,3,1:T(2,128)(2,1)} %bitcast.6) | data formatting | bytes 786432 | tf_op jit(solution)/shard_map/transpose | solution.py:448
  2.5 49.8 %pod_tensor.1 = (f32[16,512]{1,0:T(8,128)}, f32[2,1024]{1,0:T(2,128)}) custom-call(bf16[2,12,64,128]{3,2,1,0:T(8,128)(2,1)} %bitcast.5, s32[4,2,128]{2,1,0:T(2,128)} %slab_ref.1, f32[8]{0:T(128)} %vol_ref.1, s32[8]{0:T(128)} %adv_ref.1, s32[1,2048]{1,0:T(1,128)} %bitcast.7, s32[1,2048]{1,0:T(1,128)} %bitcast.8, f32[2048,1024]{1,0:T(8,128)} %amp_hbm.1), custom_call_target="tpu_custom_call" | custom-call | tf_op jit(solution)/shard_map/pod_tensor/pallas_call | solution.py:453
  52.3 1.4 %finish.1 = (f32[16,512]{1,0:T(8,128)}, f32[2,1024]{1,0:T(2,128)}) custom-call(f32[16,512]{1,0:T(8,128)} %get-tuple-element.6.tensor_ref, f32[2,1024]{1,0:T(2,128)} %get-tuple-element.7.response_ref), custom_call_target="tpu_custom_call" | custom-call | tf_op jit(solution)/shard_map/finish/pallas_call | solution.py:495
